TPU v7x, 128 devices: a whole 4x4x4 slice. The times are simulated.
128 devices in a mesh: row: 16 (over x_lo, y, core), col: 8 (over x_hi, z).
Axes of the slice: x: 4 (x_hi: 2, x_lo: 2; x = x_hi * 2 + x_lo), y: 4, z: 4, core: 2. Of those that a mesh axis runs over, the one named last changes fastest.
Arguments:
- nodes: bfloat16 [32768, 256], P(('row', 'col')), may hold values from -6 to 6
- weight: bfloat16 [256, 256], replicated, may hold values from -0.375 to 0.375
- adjacency: bfloat16 [32768, 32768], P('row', 'col'), may hold values from -0.046875 to 0.046875
- history: bfloat16 [131072, 256], P(('row', 'col')), may hold values from -6 to 6
- pull_owner: int32 [4096, 1], P(('row', 'col')), may hold values from 0 to 15; in each aligned block of 32 rows (0 to 31, 32 to 63, ...) at most 4 rows name the same one
- pull_slot: int32 [4096], P(('row', 'col')), may hold values from 0 to 7
- pull_target: int32 [4096], P(('row', 'col')), may hold values from 0 to 15
- hist_tiles: bfloat16 [4096, 128, 128], P(('row', 'col')), may hold values from -0.375 to 0.375
- cotangent: bfloat16 [32768, 256], P(('row', 'col')), may hold values from -6 to 6
Outputs:
- activated: bfloat16 [32768, 256], P(('row', 'col'))
- grad_nodes: bfloat16 [32768, 256], P(('row', 'col'))
- grad_weight: float32 [256, 256], replicated
Inputs may be any that keep to these rules, and one draw needn't show every extreme that they name: `pull_owner`: among the 32 pulls of one device no owner is named more than 4 times, a bound that some block reaches.
All inputs are finite; a program needn't handle non-finite values.
Results may differ from a plain program's by a relative error of at most 0.029.
Values may be sent and summed in bfloat16 or wider, within the bound.
A program may use at most 128 MiB of HBM per device.

v0:
```python
import math
import jax
import jax.numpy as jnp
from jax import lax
from jax.sharding import PartitionSpec as P

HID = 256
BLK = 128


def local(
    nodes, weight, adjacency, history, pull_owner, pull_slot, pull_target, hist_tiles, cotangent
):
    projected = jnp.dot(nodes, weight, preferred_element_type=jnp.float32).astype(jnp.bfloat16)
    gathered = lax.all_gather(projected, "row", axis=0, tiled=True)
    owners = pull_owner[:, 0]
    blocks = history.reshape(-1, BLK, HID)
    everything = lax.all_gather(blocks, "row", axis=0, tiled=True)
    pulled = everything[owners * blocks.shape[0] + pull_slot]
    products = jnp.einsum("kab,kbf->kaf", hist_tiles, pulled, preferred_element_type=jnp.float32)
    row_count = adjacency.shape[0] // BLK
    placing = (pull_target[None, :] == jnp.arange(row_count, dtype=jnp.int32)[:, None]).astype(
        jnp.float32
    )
    history_term = jnp.einsum(
        "jk,kaf->jaf", placing, products, precision=lax.Precision.HIGHEST
    ).reshape(-1, HID)
    in_batch = jnp.dot(adjacency, gathered, preferred_element_type=jnp.float32)
    mixed = lax.psum_scatter(
        (in_batch + history_term).astype(jnp.bfloat16), "col", scatter_dimension=0, tiled=True
    ).astype(jnp.float32)
    activated = jax.nn.silu(mixed).astype(jnp.bfloat16)
    sigmoid_z = jax.nn.sigmoid(mixed)
    grad_pre = (
        cotangent.astype(jnp.float32) * sigmoid_z * (1.0 + mixed * (1.0 - sigmoid_z))
    ).astype(jnp.bfloat16)
    grad_panel = lax.all_gather(grad_pre, "col", axis=0, tiled=True)
    grad_proj = lax.psum_scatter(
        lax.dot_general(
            adjacency, grad_panel, (((0,), (0,)), ((), ())), preferred_element_type=jnp.float32
        ).astype(jnp.bfloat16),
        "row",
        scatter_dimension=0,
        tiled=True,
    )
    grad_nodes = jnp.dot(grad_proj, weight.T, preferred_element_type=jnp.float32).astype(
        jnp.bfloat16
    )
    partial_grad = lax.dot_general(
        nodes, grad_proj, (((0,), (0,)), ((), ())), preferred_element_type=jnp.float32
    )
    all_nodes = nodes.shape[0] * lax.axis_size("row") * lax.axis_size("col")
    grad_weight = lax.psum(partial_grad, ("row", "col")) * (1.0 / math.sqrt(all_nodes))
    return (activated, grad_nodes, grad_weight)


def solution(mesh):
    return jax.shard_map(
        local,
        mesh=mesh,
        in_specs=(
            P(("row", "col"), None),
            P(),
            P("row", "col"),
            P(("row", "col"), None),
            P(("row", "col"), None),
            P(("row", "col")),
            P(("row", "col")),
            P(("row", "col"), None, None),
            P(("row", "col"), None),
        ),
        out_specs=(P(("row", "col"), None), P(("row", "col"), None), P()),
        check_vma=False,
    )
```

profile of v0, /device:TPU:1, one launch (start us, length us, event | category | flops | bytes accessed | tf_op | source)
XLA Modules:
  0.0 462.5 jit_solution(4636149198428322566)
XLA Ops:
  7.2 0.0 copy-start
  7.2 0.0 all-gather.6.cloned.1.call-start
  7.2 0.7 all-gather.6.cloned.1.call-update
  7.9 0.0 all-gather.4.cloned.1.call-start
  8.0 1.8 convolution_convert_fusion.2
  9.8 0.0 all-gather.4.cloned.1.call-update
  9.8 0.0 reduce-scatter.3.cloned.1.call-start
  9.8 0.7 compare_select_fusion
  10.5 54.9 %all-gather.6.cloned.1.call-done = bf16[128,128,256]{2,1,0:T(8,128)(2,1)} async-done(((bf16[8,128,256]{2,1,0:T(8,128)(2,1)}), bf16[128,128,256]{2,1,0:T(8,128)(2,1)}) %all-gather.6.cloned.1.call-update) | async-done | bytes 8388624 | tf_op jit(solution)/shard_map/all_gather | solution.py:18
  65.5 4.1 gather_fusion
  69.5 0.0 copy-done
  69.6 0.0 copy-start.4
  69.6 0.8 convolution_bitcast_fusion.1
  70.3 0.0 copy-done.4
  70.3 3.9 fusion.1
  74.3 28.5 %all-gather.4.cloned.1.call-done = bf16[4096,256]{1,0:T(8,128)(2,1)} async-done(((bf16[256,256]{1,0:T(8,128)(2,1)}), bf16[4096,256]{1,0:T(8,128)(2,1)}) %all-gather.4.cloned.1.call-update) | async-done | bytes 2097168 | tf_op jit(solution)/shard_map/all_gather | solution.py:15
  102.8 0.0 copy-start.3
  102.8 12.5 %fusion.4 = bf16[2048,256]{0,1:T(8,128)(2,1)} fusion(bf16[4096,256]{1,0:T(8,128)(2,1)} %all-gather.4.cloned.1.call-done, bf16[2048,4096]{1,0:T(8,128)(2,1)} %param.11, f32[32,8,16,128]{3,2,1,0:T(8,128)S(1)} %bitcast.38), kind=kOutput, calls=%fused_computation.7 | convolution fusion | flops 4296015872 | bytes 22020096 | tf_op jit(solution)/shard_map/dot_general | solution.py:28
  115.3 0.0 reduce-scatter.3.cloned.1.call-update
  115.3 0.0 all-gather.8.cloned.1.call-start
  115.3 0.0 copy-done.3
  115.4 0.1 copy.17
  115.5 69.4 %reduce-scatter.3.cloned.1.call-done = bf16[256,256]{0,1:T(8,128)(2,1)} async-done(((bf16[2048,256]{0,1:T(8,128)(2,1)}), bf16[256,256]{0,1:T(8,128)(2,1)}) %reduce-scatter.3.cloned.1.call-update) | async-done | bytes 131088 | tf_op jit(solution)/shard_map/reduce_scatter | solution.py:29
  184.9 1.7 fusion.11
  186.6 0.0 all-gather.8.cloned.1.call-update
  186.6 0.2 reduce-scatter.5.cloned.1.call-start
  186.8 46.5 %all-gather.8.cloned.1.call-done = bf16[2048,256]{0,1:T(8,128)(2,1)} async-done(((bf16[256,256]{0,1:T(8,128)(2,1)}), bf16[2048,256]{0,1:T(8,128)(2,1)}) %all-gather.8.cloned.1.call-update) | async-done | bytes 1048592 | tf_op jit(solution)/shard_map/all_gather | solution.py:37
  233.3 11.9 %fusion = bf16[4096,256]{0,1:T(8,128)(2,1)} fusion(bf16[2048,256]{0,1:T(8,128)(2,1)} %all-gather.8.cloned.1.call-done, bf16[2048,4096]{1,0:T(8,128)(2,1)} %param.11), kind=kOutput, calls=%fused_computation.2 | convolution fusion | flops 4296015872 | bytes 19922944 | tf_op jit(solution)/shard_map/dot_general | solution.py:39
  245.2 0.0 copy-start.2
  245.2 0.0 copy-start.1
  245.2 0.0 reduce-scatter.5.cloned.1.call-update
  245.3 0.0 all-reduce.2.cloned.1.call-start
  245.3 0.8 copy.18
  246.1 58.0 %reduce-scatter.5.cloned.1.call-done = bf16[256,256]{0,1:T(8,128)(2,1)} async-done(((bf16[4096,256]{0,1:T(8,128)(2,1)}), bf16[256,256]{0,1:T(8,128)(2,1)}) %reduce-scatter.5.cloned.1.call-update) | async-done | bytes 131088 | tf_op jit(solution)/shard_map/reduce_scatter | solution.py:38
  304.1 0.0 copy-done.2
  304.1 1.8 convolution_bitcast_fusion.2
  305.9 0.0 all-reduce.2.cloned.1.call-update
  305.9 0.0 copy-done.1
  305.9 1.8 convolution_convert_fusion.1
  307.7 146.1 %all-reduce.2.cloned.1.call-done = f32[256,256]{0,1:T(8,128)} async-done(((f32[256,256]{0,1:T(8,128)}), f32[256,256]{0,1:T(8,128)}) %all-reduce.2.cloned.1.call-update) | async-done | bytes 262160 | tf_op jit(solution)/shard_map/psum | solution.py:53
  453.8 1.0 broadcast_multiply_fusion
  454.8 0.8 copy.19
  (1 shorter events, 0.0 us)
Async XLA Ops:
  7.2 62.4 %copy-start = (bf16[32,128,128]{2,1,0:T(8,128)(2,1)S(1)}, bf16[32,128,128]{2,1,0:T(8,128)(2,1)}, u32[]{:S(2)}) copy-start(bf16[32,128,128]{2,1,0:T(8,128)(2,1)} %param.16) | copy-start | bytes 3145732
  7.2 58.3 %all-gather.6.cloned.1.call-start = ((), (), s32[]{:S(2)}) async-start(), calls=%async_computation.3 | async-start | bytes 8912896 | tf_op jit(solution)/shard_map/all_gather | solution.py:18
  7.9 94.9 %all-gather.4.cloned.1.call-start = ((), (), s32[]{:S(2)}) async-start(), calls=%async_computation.2 | async-start | bytes 2228224 | tf_op jit(solution)/shard_map/all_gather | solution.py:15
  9.8 175.1 %reduce-scatter.3.cloned.1.call-start = ((), (), s32[]{:S(2)}) async-start(), calls=%async_computation.4 | async-start | bytes 1179648 | tf_op jit(solution)/shard_map/reduce_scatter | solution.py:29
  69.6 0.8 copy-start.4
  102.8 12.6 %copy-start.3 = (bf16[256,256]{1,0:T(8,128)(2,1)S(1)}, bf16[256,256]{1,0:T(8,128)(2,1)}, u32[]{:S(2)}) copy-start(bf16[256,256]{1,0:T(8,128)(2,1)} %param.17) | copy-start | bytes 393220
  115.3 118.0 %all-gather.8.cloned.1.call-start = ((), (), s32[]{:S(2)}) async-start(), calls=%async_computation.5 | async-start | bytes 1179648 | tf_op jit(solution)/shard_map/all_gather | solution.py:37
  186.6 117.4 %reduce-scatter.5.cloned.1.call-start = ((), (), s32[]{:S(2)}) async-start(), calls=%async_computation.6 | async-start | bytes 2228224 | tf_op jit(solution)/shard_map/reduce_scatter | solution.py:38
  245.2 58.8 %copy-start.2 = (bf16[256,256]{1,0:T(8,128)(2,1)S(1)}, bf16[256,256]{1,0:T(8,128)(2,1)}, u32[]{:S(2)}) copy-start(bf16[256,256]{1,0:T(8,128)(2,1)} %param.9) | copy-start | bytes 393220
  245.2 60.6 %copy-start.1 = (bf16[256,256]{1,0:T(8,128)(2,1)S(1)}, bf16[256,256]{1,0:T(8,128)(2,1)}, u32[]{:S(2)}) copy-start(bf16[256,256]{1,0:T(8,128)(2,1)} %param.10) | copy-start | bytes 393220
  245.3 208.5 %all-reduce.2.cloned.1.call-start = ((), (), s32[]{:S(2)}) async-start(), calls=%async_computation.7 | async-start | bytes 524288 | tf_op jit(solution)/shard_map/psum | solution.py:53
Sparse Core Ops, SparseCore 0:
  9.7 55.7 all-gather.5
  67.7 34.9 all-gather.3
  115.4 69.4 reduce-scatter.2
  187.7 45.5 all-gather.7
  245.4 58.6 reduce-scatter.4
  310.0 143.8 all-reduce.1
where the time goes:
time: 463 us; the launch traced here: 462 us
  waiting for transfers between devices  404 us (87%)
  matrix products  34.5 us (7%)
  between operations  14.2 us (3%)
  local copies, waits for them, and re-layouts  5.78 us (1%)
    psum x1, waiting for transfers between devices, local(): lax.psum(partial_grad, ('row', 'col')) * (1.0 / math.sqrt(all_nodes))  146 us
    reduce_scatter x1, waiting for transfers between devices, local(): lax.psum_scatter((in_batch + history_term).astype(jnp.bfloat16), 'col', s...  69.4 us
    reduce_scatter x1, waiting for transfers between devices, local(): lax.psum_scatter(lax.dot_general(adjacency, grad_panel, (((0,), (0,)), ((...  58 us
    all_gather x1, waiting for transfers between devices, local(): everything = lax.all_gather(blocks, 'row', axis=0, tiled=True)  54.9 us
    all_gather x1, waiting for transfers between devices, local(): grad_panel = lax.all_gather(grad_pre, 'col', axis=0, tiled=True)  46.5 us
    all_gather x1, waiting for transfers between devices, local(): gathered = lax.all_gather(projected, 'row', axis=0, tiled=True)  28.5 us
    dot_general x1, matrix products, local(): in_batch = jnp.dot(adjacency, gathered, preferred_element_type=jnp.float32)  12.5 us
    dot_general x1, matrix products, local(): lax.dot_general(adjacency, grad_panel, (((0,), (0,)), ((), ())), preferre...  11.9 us
  transfers between devices with their start and end apart: 6, of which 6 were waited for; matrix products, arithmetic and copies ran while one was open for 3% of the time, Pallas kernels for 0%

commit v1 on v0

--- a/solution.py
+++ b/solution.py
@@ -50,7 +50,9 @@
         nodes, grad_proj, (((0,), (0,)), ((), ())), preferred_element_type=jnp.float32
     )
     all_nodes = nodes.shape[0] * lax.axis_size("row") * lax.axis_size("col")
-    grad_weight = lax.psum(partial_grad, ("row", "col")) * (1.0 / math.sqrt(all_nodes))
+    grad_weight = jnp.sum(lax.all_gather(partial_grad, ("row", "col")), axis=0) * (
+        1.0 / math.sqrt(all_nodes)
+    )
     return (activated, grad_nodes, grad_weight)
 
 

time: 463 us -> 689 us (1.49)
  waiting for transfers between devices: 404 us -> 608 us
  local copies, waits for them, and re-layouts: 5.78 us -> 25.4 us
    all_gather x0 -> x1, waiting for transfers between devices: none -> 349 us  [local(): lax.all_gather(partial_grad, ('row', 'col'))]
    psum x1 -> x0, waiting for transfers between devices: 146 us -> none  [local(): lax.psum(partial_grad, ('row', 'col')) * (1.0 / math.sqrt(all_nodes))]
    unnamed x13 -> x16, local copies, waits for them, and re-layouts: 1.72 us -> 21.3 us
  transfers between devices with their start and end apart: 6 -> 6, of which waited for: 6 -> 6; matrix products, arithmetic and copies ran while one was open for 3% -> 2% of each run, Pallas kernels for 0% -> 0%
where the time goes in v1:
time: 689 us
  waiting for transfers between devices  608 us (88%)
  matrix products  34.5 us (5%)
  local copies, waits for them, and re-layouts  25.4 us (4%)
  between operations  14.2 us (2%)
    all_gather x1, waiting for transfers between devices, local(): lax.all_gather(partial_grad, ('row', 'col'))  349 us
    reduce_scatter x1, waiting for transfers between devices, local(): lax.psum_scatter((in_batch + history_term).astype(jnp.bfloat16), 'col', s...  69.5 us
    reduce_scatter x1, waiting for transfers between devices, local(): lax.psum_scatter(lax.dot_general(adjacency, grad_panel, (((0,), (0,)), ((...  58.7 us
    all_gather x1, waiting for transfers between devices, local(): everything = lax.all_gather(blocks, 'row', axis=0, tiled=True)  54.9 us
    all_gather x1, waiting for transfers between devices, local(): grad_panel = lax.all_gather(grad_pre, 'col', axis=0, tiled=True)  46.4 us
    all_gather x1, waiting for transfers between devices, local(): gathered = lax.all_gather(projected, 'row', axis=0, tiled=True)  28.5 us
    unnamed x16, local copies, waits for them, and re-layouts  21.3 us
  transfers between devices with their start and end apart: 6, of which 6 were waited for; matrix products, arithmetic and copies ran while one was open for 2% of the time, Pallas kernels for 0%

profile of v1, /device:TPU:1, one launch (start us, length us, event | category | flops | bytes accessed | tf_op | source)
XLA Modules:
  0.0 689.0 jit_solution(17232893076609915504)
XLA Ops:
  7.2 0.0 copy-start
  7.2 0.0 all-gather.8.cloned.1.call-start
  7.2 0.7 all-gather.8.cloned.1.call-update
  7.9 0.0 all-gather.6.cloned.1.call-start
  8.0 1.8 convolution_convert_fusion.2
  9.8 0.0 all-gather.6.cloned.1.call-update
  9.8 0.0 reduce-scatter.3.cloned.1.call-start
  9.8 0.7 compare_select_fusion
  10.5 54.9 %all-gather.8.cloned.1.call-done = bf16[128,128,256]{2,1,0:T(8,128)(2,1)} async-done(((bf16[8,128,256]{2,1,0:T(8,128)(2,1)}), bf16[128,128,256]{2,1,0:T(8,128)(2,1)}) %all-gather.8.cloned.1.call-update) | async-done | bytes 8388624 | tf_op jit(solution)/shard_map/all_gather | solution.py:18
  65.5 4.1 gather_fusion
  69.5 0.0 copy-done
  69.6 0.0 copy-start.5
  69.6 0.8 convolution_bitcast_fusion.1
  70.3 0.0 copy-done.5
  70.3 3.9 fusion.1
  74.3 28.5 %all-gather.6.cloned.1.call-done = bf16[4096,256]{1,0:T(8,128)(2,1)} async-done(((bf16[256,256]{1,0:T(8,128)(2,1)}), bf16[4096,256]{1,0:T(8,128)(2,1)}) %all-gather.6.cloned.1.call-update) | async-done | bytes 2097168 | tf_op jit(solution)/shard_map/all_gather | solution.py:15
  102.8 0.0 copy-start.4
  102.8 12.5 %fusion.4 = bf16[2048,256]{0,1:T(8,128)(2,1)} fusion(bf16[4096,256]{1,0:T(8,128)(2,1)} %all-gather.6.cloned.1.call-done, bf16[2048,4096]{1,0:T(8,128)(2,1)} %param.11, f32[32,8,16,128]{3,2,1,0:T(8,128)S(1)} %bitcast.44), kind=kOutput, calls=%fused_computation.8 | convolution fusion | flops 4296015872 | bytes 22020096 | tf_op jit(solution)/shard_map/dot_general | solution.py:28
  115.3 0.0 reduce-scatter.3.cloned.1.call-update
  115.3 0.0 all-gather.10.cloned.1.call-start
  115.3 0.0 copy-done.4
  115.4 0.1 copy.16
  115.5 69.5 %reduce-scatter.3.cloned.1.call-done = bf16[256,256]{0,1:T(8,128)(2,1)} async-done(((bf16[2048,256]{0,1:T(8,128)(2,1)}), bf16[256,256]{0,1:T(8,128)(2,1)}) %reduce-scatter.3.cloned.1.call-update) | async-done | bytes 131088 | tf_op jit(solution)/shard_map/reduce_scatter | solution.py:29
  185.0 1.7 fusion.11
  186.6 0.0 all-gather.10.cloned.1.call-update
  186.7 0.0 copy-start.3
  186.7 0.0 copy-start.2
  186.7 0.2 reduce-scatter.5.cloned.1.call-start
  186.9 46.4 %all-gather.10.cloned.1.call-done = bf16[2048,256]{0,1:T(8,128)(2,1)} async-done(((bf16[256,256]{0,1:T(8,128)(2,1)}), bf16[2048,256]{0,1:T(8,128)(2,1)}) %all-gather.10.cloned.1.call-update) | async-done | bytes 1048592 | tf_op jit(solution)/shard_map/all_gather | solution.py:37
  233.3 11.9 %fusion = bf16[4096,256]{0,1:T(8,128)(2,1)} fusion(bf16[2048,256]{0,1:T(8,128)(2,1)} %all-gather.10.cloned.1.call-done, bf16[2048,4096]{1,0:T(8,128)(2,1)} %param.11), kind=kOutput, calls=%fused_computation.3 | convolution fusion | flops 4296015872 | bytes 19922944 | tf_op jit(solution)/shard_map/dot_general | solution.py:39
  245.2 0.0 reduce-scatter.5.cloned.1.call-update
  245.2 0.0 all-gather.12.cloned.1.call-start
  245.3 58.7 %reduce-scatter.5.cloned.1.call-done = bf16[256,256]{0,1:T(8,128)(2,1)} async-done(((bf16[4096,256]{0,1:T(8,128)(2,1)}), bf16[256,256]{0,1:T(8,128)(2,1)}) %reduce-scatter.5.cloned.1.call-update) | async-done | bytes 131088 | tf_op jit(solution)/shard_map/reduce_scatter | solution.py:38
  304.0 0.0 copy-done.3
  304.0 1.8 convolution_bitcast_fusion.2
  305.8 0.0 all-gather.12.cloned.1.call-update
  305.9 0.8 copy.17
  306.6 0.0 copy-done.2
  306.6 1.8 convolution_convert_fusion.1
  308.4 349.1 %all-gather.12.cloned.1.call-done = f32[32768,256]{0,1:T(8,128)} async-done(((f32[256,256]{0,1:T(8,128)}), f32[32768,256]{0,1:T(8,128)}) %all-gather.12.cloned.1.call-update) | async-done | bytes 33554448 | tf_op jit(solution)/shard_map/all_gather | solution.py:53
  657.5 19.6 %copy.24 = f32[32,8,128,256]{3,2,1,0:T(8,128)S(1)} copy(f32[32,8,128,256]{3,1,2,0:T(8,128)} %bitcast.43) | data formatting | bytes 67108864
  677.1 0.0 copy-start.1
  677.1 4.1 bitcast_reduce_fusion
  681.3 0.8 copy.18
  682.1 0.0 copy-done.1
  (2 shorter events, 0.0 us)
Async XLA Ops:
  7.2 62.4 %copy-start = (bf16[32,128,128]{2,1,0:T(8,128)(2,1)S(1)}, bf16[32,128,128]{2,1,0:T(8,128)(2,1)}, u32[]{:S(2)}) copy-start(bf16[32,128,128]{2,1,0:T(8,128)(2,1)} %param.16) | copy-start | bytes 3145732
  7.2 58.3 %all-gather.8.cloned.1.call-start = ((), (), s32[]{:S(2)}) async-start(), calls=%async_computation.3 | async-start | bytes 8912896 | tf_op jit(solution)/shard_map/all_gather | solution.py:18
  7.9 94.9 %all-gather.6.cloned.1.call-start = ((), (), s32[]{:S(2)}) async-start(), calls=%async_computation.2 | async-start | bytes 2228224 | tf_op jit(solution)/shard_map/all_gather | solution.py:15
  9.8 175.2 %reduce-scatter.3.cloned.1.call-start = ((), (), s32[]{:S(2)}) async-start(), calls=%async_computation.4 | async-start | bytes 1179648 | tf_op jit(solution)/shard_map/reduce_scatter | solution.py:29
  69.6 0.8 copy-start.5
  102.8 12.6 %copy-start.4 = (bf16[256,256]{1,0:T(8,128)(2,1)S(1)}, bf16[256,256]{1,0:T(8,128)(2,1)}, u32[]{:S(2)}) copy-start(bf16[256,256]{1,0:T(8,128)(2,1)} %param.17) | copy-start | bytes 393220
  115.3 118.0 %all-gather.10.cloned.1.call-start = ((), (), s32[]{:S(2)}) async-start(), calls=%async_computation.5 | async-start | bytes 1179648 | tf_op jit(solution)/shard_map/all_gather | solution.py:37
  186.7 117.4 %copy-start.3 = (bf16[256,256]{1,0:T(8,128)(2,1)S(1)}, bf16[256,256]{1,0:T(8,128)(2,1)}, u32[]{:S(2)}) copy-start(bf16[256,256]{1,0:T(8,128)(2,1)} %param.9) | copy-start | bytes 393220
  186.7 119.9 %copy-start.2 = (bf16[256,256]{1,0:T(8,128)(2,1)S(1)}, bf16[256,256]{1,0:T(8,128)(2,1)}, u32[]{:S(2)}) copy-start(bf16[256,256]{1,0:T(8,128)(2,1)} %param.10) | copy-start | bytes 393220
  186.7 117.3 %reduce-scatter.5.cloned.1.call-start = ((), (), s32[]{:S(2)}) async-start(), calls=%async_computation.6 | async-start | bytes 2228224 | tf_op jit(solution)/shard_map/reduce_scatter | solution.py:38
  245.2 412.3 %all-gather.12.cloned.1.call-start = ((), (), s32[]{:S(2)}) async-start(), calls=%async_computation.7 | async-start | bytes 33816576 | tf_op jit(solution)/shard_map/all_gather | solution.py:53
  677.1 5.0 copy-start.1
Sparse Core Ops, SparseCore 0:
  9.7 55.7 all-gather.7
  67.8 34.9 all-gather.5
  115.4 69.5 reduce-scatter.2
  187.8 45.4 all-gather.9
  245.4 58.6 reduce-scatter.4
  306.3 351.2 all-gather.11
